TPU v7x, 512 devices: a whole 4x8x8 slice. The times are simulated.
512 devices in a mesh: expert: 8 (over y), tensor: 64 (over z, x, core).
Axes of the slice: x: 4, y: 8, z: 8, core: 2. Of those that a mesh axis runs over, the one named last changes fastest.
Arguments:
- expert_hidden: bfloat16 [8, 768, 8192], P('expert', 'tensor'), may hold values from -6 to 6
- probe_tangent: bfloat16 [8, 6144, 8192], P('expert', 'tensor'), may hold values from -0.0625 to 0.0625
- routed_experts: int32 [1536, 2], P('expert'), may hold values from 0 to 7, all different within a row; in each aligned block of 192 rows (0 to 191, 192 to 383, ...) at most 96 rows name the same one
- gate_weights: float32 [1536, 2], P('expert'), may hold values from 0.1 to 1
Outputs:
- ggn_product: bfloat16 [8, 6144, 8192], P('expert', 'tensor')
- token_quadratic: float32 [1536], P('expert')
Inputs may be any that keep to these rules, and one draw needn't show every extreme that they name: `routed_experts`: each row names two different experts. Among the 192 rows of one source, no expert is named by more than 96 rows, a bound that some block reaches.
All inputs are finite; a program needn't handle non-finite values.
Results may differ from a plain program's by a relative error of at most 0.0057.
Values may be sent and summed in bfloat16 or wider, within the bound.
No kernel may reach another device: no remote copies, remote signals or barrier semaphores. Data moves between devices by JAX's collectives and lax.ppermute only.
A program may use at most 128 MiB of HBM per device.

v0:
```python
import jax
import jax.numpy as jnp
from jax import lax
from jax.sharding import PartitionSpec as P


def local(expert_hidden, probe_tangent, routed_experts, gate_weights):
    expert_count = lax.axis_size("expert")
    tensor_count = lax.axis_size("tensor")
    hidden_local = expert_hidden[0]
    probe_local = probe_tangent[0]
    col_count = probe_local.shape[0]
    tok_count = routed_experts.shape[0]
    capacity = hidden_local.shape[0] * tensor_count // expert_count
    ids_flat = routed_experts.reshape(-1)
    gate_flat = gate_weights.reshape(-1)
    one_hot = (ids_flat[:, None] == jnp.arange(expert_count, dtype=jnp.int32)[None, :]).astype(
        jnp.int32
    )
    earlier = jnp.cumsum(one_hot, axis=0) - one_hot
    slot_rank = jnp.sum(one_hot * earlier, axis=1)
    buffer_row = ids_flat * capacity + slot_rank
    hidden_all = lax.all_gather(hidden_local, "tensor", axis=0, tiled=True)
    expert_tangent = lax.dot_general(
        hidden_all, probe_local, (((1,), (1,)), ((), ())), preferred_element_type=jnp.float32
    ).astype(jnp.bfloat16)
    outgoing = expert_tangent.reshape(expert_count, capacity, col_count)
    received = lax.all_to_all(outgoing, "expert", split_axis=0, concat_axis=0, tiled=True)
    block_cols = received.shape[2]
    flat_rows = received.reshape(expert_count * capacity, block_cols)
    picked = flat_rows[buffer_row].astype(jnp.float32) * gate_flat[:, None]
    token_tangent = jnp.sum(picked.reshape(tok_count, 2, block_cols), axis=1)
    weighted = (token_tangent[:, None, :] * gate_weights[:, :, None]).reshape(
        tok_count * 2, block_cols
    )
    weighted = weighted.astype(jnp.bfloat16)
    buffer = (
        jnp.zeros((expert_count * capacity, block_cols), jnp.bfloat16).at[buffer_row].set(weighted)
    )
    buffer, token_tangent = (buffer, token_tangent)
    returning = lax.all_to_all(
        buffer.reshape(expert_count, capacity, col_count),
        "expert",
        split_axis=0,
        concat_axis=0,
        tiled=True,
    )
    returning_flat = returning.reshape(expert_count * capacity, col_count)
    gradient = lax.dot_general(
        returning_flat, hidden_all, (((0,), (0,)), ((), ())), preferred_element_type=jnp.float32
    ).astype(jnp.bfloat16)
    partial_squares = jnp.sum(token_tangent * token_tangent, axis=1)
    total_squares = lax.psum(partial_squares, "tensor")
    token_quadratic = total_squares / (col_count * tensor_count)
    return (gradient[None], token_quadratic)


def solution(mesh):
    placed = (
        P("expert", "tensor", None),
        P("expert", "tensor", None),
        P("expert", None),
        P("expert", None),
    )
    return jax.shard_map(
        local,
        mesh=mesh,
        in_specs=placed,
        out_specs=(P("expert", "tensor", None), P("expert")),
        check_vma=False,
    )
```

profile of v0, /device:TPU:1, one launch (start us, length us, event | category | flops | bytes accessed | tf_op | source)
XLA Modules:
  0.0 347.5 jit_solution(15207525154912715444)
XLA Ops:
  7.2 0.0 copy-start
  7.2 0.0 copy-start.1
  7.2 0.0 all-gather.3.cloned.1.call-start
  7.2 2.1 copy.33
  9.4 0.0 all-gather.3.cloned.1.call-update
  9.4 0.8 copy.31
  10.2 0.1 eq.29
  10.3 0.1 eq.25
  10.5 0.9 reduce-window.6
  11.4 0.2 slice_reduce_fusion
  11.6 0.7 broadcast_multiply_fusion
  12.3 132.1 %all-gather.3.cloned.1.call-done = bf16[1,768,8192]{2,0,1:T(2,128)(2,1)} async-done(((bf16[1,12,8192]{2,0,1:T(2,128)(2,1)}), bf16[1,768,8192]{2,0,1:T(2,128)(2,1)}) %all-gather.3.cloned.1.call-update) | async-done | bytes 12582928 | tf_op jit(solution)/shard_map/all_gather | solution.py:23
  144.4 0.0 copy-done
  144.4 22.4 %fusion.13 = bf16[768,96]{0,1:T(8,128)(2,1)S(1)} fusion(bf16[1,96,8192]{2,1,0:T(8,128)(2,1)S(1)} %copy-done, bf16[1,768,8192]{2,0,1:T(2,128)(2,1)} %all-gather.3.cloned.1.call-done), kind=kOutput, calls=%fused_computation.11 | convolution fusion | flops 1208033280 | bytes 14303232 | tf_op jit(solution)/shard_map/dot_general | solution.py:24
  166.8 0.2 reshape.79
  167.0 0.7 copy.34
  167.7 6.5 %all-to-all-start = ((bf16[8,96,96]{1,2,0:T(8,128)(2,1)}), bf16[8,96,96]{1,2,0:T(8,128)(2,1)S(1)}, u32[]{:S(2)}, u32[]{:S(2)}) async-start(bf16[8,96,96]{1,2,0:T(8,128)(2,1)} %copy.34), calls=%async_computation | async-start | bytes 393216 | tf_op jit(solution)/shard_map/all_to_all | solution.py:28
  174.2 0.1 fusion.23
  174.3 0.1 copy.30
  174.4 0.1 mul.51
  174.5 0.0 copy-done.1
  174.6 0.1 copy.36
  174.7 0.1 mul.57
  174.9 8.9 %all-to-all-done = bf16[8,96,96]{1,2,0:T(8,128)(2,1)S(1)} async-done(((bf16[8,96,96]{1,2,0:T(8,128)(2,1)}), bf16[8,96,96]{1,2,0:T(8,128)(2,1)S(1)}, u32[]{:S(2)}, u32[]{:S(2)}) %all-to-all-start) | async-done | bytes 147488 | tf_op jit(solution)/shard_map/all_to_all | solution.py:28
  183.8 0.1 copy.35
  183.9 1.4 gather_fusion
  185.4 0.3 fusion.18
  185.7 0.1 mul.55
  185.8 2.2 scatter_custom_fusion
  188.0 3.4 all-to-all-start.1
  191.4 0.1 multiply_reduce_fusion
  191.5 125.3 %psum.7 = f32[192]{0:T(256)S(1)} all-reduce(f32[192]{0:T(256)S(1)} %multiply_reduce_fusion), channel_id=1, replica_groups=mesh['expert'=8,'tensor'=64] {'tensor'}, use_global_device_ids=true, to_apply=%region_6.7 | all-reduce | flops 192 | bytes 1536 | tf_op jit(solution)/shard_map/psum | solution.py:53
  316.8 0.6 broadcast_multiply_fusion.1
  317.3 0.0 all-to-all-done.1
  317.3 23.3 %fusion.7 = bf16[1,96,8192]{2,1,0:T(8,128)(2,1)} fusion(bf16[768,96]{1,0:T(8,128)(2,1)S(1)} %bitcast.38, bf16[1,768,8192]{2,0,1:T(2,128)(2,1)} %all-gather.3.cloned.1.call-done), kind=kOutput, calls=%fused_computation.7 | convolution fusion | flops 1208745984 | bytes 14303232 | tf_op jit(solution)/shard_map/dot_general | solution.py:49
  (4 shorter events, 0.1 us)
Async XLA Ops:
  7.2 137.2 %copy-start = (bf16[1,96,8192]{2,1,0:T(8,128)(2,1)S(1)}, bf16[1,96,8192]{2,1,0:T(8,128)(2,1)}, u32[]{:S(2)}) copy-start(bf16[1,96,8192]{2,1,0:T(8,128)(2,1)} %param.5) | copy-start | bytes 4718596
  7.2 167.4 %copy-start.1 = (f32[192,2]{0,1:T(2,128)S(1)}, f32[192,2]{0,1:T(2,128)}, u32[]{:S(2)}) copy-start(f32[192,2]{0,1:T(2,128)} %param.7) | copy-start | bytes 4612
  7.2 137.2 %all-gather.3.cloned.1.call-start = ((), (), s32[]{:S(2)}) async-start(), calls=%async_computation.2 | async-start | bytes 25559040 | tf_op jit(solution)/shard_map/all_gather | solution.py:23
  167.7 16.0 %all-to-all-start = ((bf16[8,96,96]{1,2,0:T(8,128)(2,1)}), bf16[8,96,96]{1,2,0:T(8,128)(2,1)S(1)}, u32[]{:S(2)}, u32[]{:S(2)}) async-start(bf16[8,96,96]{1,2,0:T(8,128)(2,1)} %copy.34), calls=%async_computation | async-start | bytes 393216 | tf_op jit(solution)/shard_map/all_to_all | solution.py:28
  188.0 129.3 %all-to-all-start.1 = ((bf16[8,96,96]{2,1,0:T(8,128)(2,1)}), bf16[8,96,96]{2,1,0:T(8,128)(2,1)S(1)}, u32[]{:S(2)}, u32[]{:S(2)}) async-start(bf16[8,96,96]{2,1,0:T(8,128)(2,1)} %bitcast.6), calls=%async_computation.1 | async-start | bytes 393216 | tf_op jit(solution)/shard_map/all_to_all | solution.py:41
Sparse Core Ops, SparseCore 0:
  11.9 132.4 all-gather.2
where the time goes:
time: 348 us
  waiting for transfers between devices  141 us (41%)
  blocking collectives  125 us (36%)
  matrix products  45.7 us (13%)
  between operations  14.2 us (4%)
  starting transfers between devices  9.89 us (3%)
  local copies, waits for them, and re-layouts  6.58 us (2%)
  other arithmetic  4.95 us (1%)
    all_gather x1, waiting for transfers between devices, local(): hidden_all = lax.all_gather(hidden_local, 'tensor', axis=0, tiled=True)  132 us
    psum x1, blocking collectives, local(): total_squares = lax.psum(partial_squares, 'tensor')  125 us
    dot_general x1, matrix products, local(): lax.dot_general(returning_flat, hidden_all, (((0,), (0,)), ((), ())), pre...  23.3 us
    dot_general x1, matrix products, local(): lax.dot_general(hidden_all, probe_local, (((1,), (1,)), ((), ())), prefer...  22.4 us
    all_to_all x1, waiting for transfers between devices, local(): lax.all_to_all(outgoing, 'expert', split_axis=0, concat_axis=0, tiled=True)  8.9 us
  transfers between devices with their start and end apart: 3, of which 2 were waited for; matrix products, arithmetic and copies ran while one was open for 1% of the time, Pallas kernels for 0%

commit v1 on v0

--- a/solution.py
+++ b/solution.py
@@ -20,7 +20,9 @@
     earlier = jnp.cumsum(one_hot, axis=0) - one_hot
     slot_rank = jnp.sum(one_hot * earlier, axis=1)
     buffer_row = ids_flat * capacity + slot_rank
-    hidden_all = lax.all_gather(hidden_local, "tensor", axis=0, tiled=True)
+    hidden_all = jnp.concatenate(
+        lax.all_to_all(jnp.stack([hidden_local] * lax.axis_size("tensor")), "tensor", 0, 0), axis=0
+    )
     expert_tangent = lax.dot_general(
         hidden_all, probe_local, (((1,), (1,)), ((), ())), preferred_element_type=jnp.float32
     ).astype(jnp.bfloat16)

time: 348 us -> 572 us (1.64)
  waiting for transfers between devices: 141 us -> 371 us
  matrix products: 45.7 us -> 16.5 us
  local copies, waits for them, and re-layouts: 6.58 us -> 27.4 us
  starting transfers between devices: 9.89 us -> 25.4 us
  between operations: 14.2 us -> 0.78 us
    all_to_all x0 -> x1, waiting for transfers between devices: none -> 361 us  [local(): lax.all_to_all(jnp.stack([hidden_local] * lax.axis_size('tensor')), 'tens...]
    all_gather x1 -> x0, waiting for transfers between devices: 132 us -> none  [local(): hidden_all = lax.all_gather(hidden_local, 'tensor', axis=0, tiled=True)]
    reshape x0 -> x1, local copies, waits for them, and re-layouts: none -> 16.8 us  [local(): jnp.concatenate(lax.all_to_all(jnp.stack([hidden_local] * lax.axis_size('...]
    dot_general x1, matrix products: 23.3 us -> 7.9 us  [local(): lax.dot_general(returning_flat, hidden_all, (((0,), (0,)), ((), ())), pre...]
    all_to_all x0 -> x1, starting transfers between devices: none -> 15.1 us  [local(): lax.all_to_all(jnp.stack([hidden_local] * lax.axis_size('tensor')), 'tens...]
    dot_general x1, matrix products: 22.4 us -> 8.58 us  [local(): lax.dot_general(hidden_all, probe_local, (((1,), (1,)), ((), ())), prefer...]
    another operation x0 -> x1, local copies, waits for them, and re-layouts: none -> 6.81 us  [local(): jnp.stack([hidden_local] * lax.axis_size('tensor'))]
  transfers between devices with their start and end apart: 3 -> 3, of which waited for: 2 -> 2; matrix products, arithmetic and copies ran while one was open for 1% -> 0% of each run, Pallas kernels for 0% -> 0%
where the time goes in v1:
time: 572 us; the launch traced here: 571 us
  waiting for transfers between devices  371 us (65%)
  blocking collectives  126 us (22%)
  local copies, waits for them, and re-layouts  27.4 us (5%)
  starting transfers between devices  25.4 us (4%)
  matrix products  16.5 us (3%)
    all_to_all x1, waiting for transfers between devices, local(): lax.all_to_all(jnp.stack([hidden_local] * lax.axis_size('tensor')), 'tens...  361 us
    psum x1, blocking collectives, local(): total_squares = lax.psum(partial_squares, 'tensor')  126 us
    reshape x1, local copies, waits for them, and re-layouts, local(): jnp.concatenate(lax.all_to_all(jnp.stack([hidden_local] * lax.axis_size('...  16.8 us
    all_to_all x1, starting transfers between devices, local(): lax.all_to_all(jnp.stack([hidden_local] * lax.axis_size('tensor')), 'tens...  15.1 us
  transfers between devices with their start and end apart: 3, of which 2 were waited for; matrix products, arithmetic and copies ran while one was open for 0% of the time, Pallas kernels for 0%

profile of v1, /device:TPU:1, one launch (start us, length us, event | category | flops | bytes accessed | tf_op | source)
XLA Modules:
  0.0 571.2 jit_solution(1885289066221089834)
XLA Ops:
  0.6 0.0 copy-start
  0.6 6.8 %stack.3 = bf16[64,12,8192]{2,1,0:T(8,128)(2,1)} broadcast(bf16[12,8192]{1,0:T(8,128)(2,1)} %bitcast.32), dimensions={1,2} | broadcast | bytes 12779520 | tf_op jit(solution)/shard_map/stack | solution.py:24
  7.5 0.0 copy-start.1
  7.5 15.1 %all-to-all-start = ((bf16[64,12,8192]{2,1,0:T(8,128)(2,1)}), bf16[64,12,8192]{2,1,0:T(8,128)(2,1)}, u32[]{:S(2)}, u32[]{:S(2)}) async-start(bf16[64,12,8192]{2,1,0:T(8,128)(2,1)} %stack.3), calls=%async_computation | async-start | bytes 33554432 | tf_op jit(solution)/shard_map/all_to_all | solution.py:24
  22.6 0.0 copy-done.1
  22.6 0.1 copy.22
  22.7 0.1 eq.29
  22.9 0.1 eq.25
  23.1 0.9 reduce-window.6
  23.9 0.2 slice_reduce_fusion
  24.2 361.0 %all-to-all-done = bf16[64,12,8192]{2,1,0:T(8,128)(2,1)} async-done(((bf16[64,12,8192]{2,1,0:T(8,128)(2,1)}), bf16[64,12,8192]{2,1,0:T(8,128)(2,1)}, u32[]{:S(2)}, u32[]{:S(2)}) %all-to-all-start) | async-done | bytes 12582944 | tf_op jit(solution)/shard_map/all_to_all | solution.py:24
  385.1 16.8 %reshape.83 = bf16[768,8192]{1,0:T(8,128)(2,1)} reshape(bf16[64,12,8192]{2,1,0:T(8,128)(2,1)} %all-to-all-done) | data formatting | bytes 25165824 | tf_op jit(solution)/shard_map/reshape | solution.py:23
  402.0 0.0 copy-done
  402.0 0.0 copy-start.2
  402.0 8.6 %fusion.3 = bf16[768,96]{0,1:T(8,128)(2,1)S(1)} fusion(bf16[768,8192]{1,0:T(8,128)(2,1)} %reshape.83, bf16[1,96,8192]{2,1,0:T(8,128)(2,1)S(1)} %copy-done), kind=kOutput, calls=%fused_computation.6 | convolution fusion | flops 1208033280 | bytes 14303232 | tf_op jit(solution)/shard_map/dot_general | solution.py:26
  410.6 0.2 reshape.84
  410.8 0.7 copy.24
  411.5 6.8 %all-to-all-start.1 = ((bf16[8,96,96]{1,2,0:T(8,128)(2,1)}), bf16[8,96,96]{1,2,0:T(8,128)(2,1)S(1)}, u32[]{:S(2)}, u32[]{:S(2)}) async-start(bf16[8,96,96]{1,2,0:T(8,128)(2,1)} %copy.24), calls=%async_computation.1 | async-start | bytes 393216 | tf_op jit(solution)/shard_map/all_to_all | solution.py:30
  418.3 0.1 fusion.11
  418.4 0.1 copy.21
  418.6 0.1 mul.51
  418.7 0.0 copy-done.2
  418.7 0.1 copy.26
  418.8 0.1 mul.57
  419.0 10.2 %all-to-all-done.1 = bf16[8,96,96]{1,2,0:T(8,128)(2,1)S(1)} async-done(((bf16[8,96,96]{1,2,0:T(8,128)(2,1)}), bf16[8,96,96]{1,2,0:T(8,128)(2,1)S(1)}, u32[]{:S(2)}, u32[]{:S(2)}) %all-to-all-start.1) | async-done | bytes 147488 | tf_op jit(solution)/shard_map/all_to_all | solution.py:30
  429.2 0.1 copy.25
  429.3 1.4 gather_fusion
  430.8 0.3 fusion.6
  431.2 0.1 mul.55
  431.2 2.2 scatter_custom_fusion
  433.4 3.4 all-to-all-start.2
  436.8 0.1 multiply_reduce_fusion
  437.0 125.8 %psum.7 = f32[192]{0:T(256)S(1)} all-reduce(f32[192]{0:T(256)S(1)} %multiply_reduce_fusion), channel_id=1, replica_groups=mesh['expert'=8,'tensor'=64] {'tensor'}, use_global_device_ids=true, to_apply=%region_6.7 | all-reduce | flops 192 | bytes 1536 | tf_op jit(solution)/shard_map/psum | solution.py:55
  562.7 0.6 broadcast_multiply_fusion.1
  563.3 0.0 all-to-all-done.2
  563.3 7.9 %fusion = bf16[1,96,8192]{2,1,0:T(8,128)(2,1)} fusion(bf16[768,96]{1,0:T(8,128)(2,1)S(1)} %bitcast.29, bf16[768,8192]{1,0:T(8,128)(2,1)} %reshape.83), kind=kOutput, calls=%fused_computation.3 | convolution fusion | flops 1208745984 | bytes 14303232 | tf_op jit(solution)/shard_map/dot_general | solution.py:51
  (5 shorter events, 0.1 us)
Async XLA Ops:
  0.6 401.4 %copy-start = (bf16[1,96,8192]{2,1,0:T(8,128)(2,1)S(1)}, bf16[1,96,8192]{2,1,0:T(8,128)(2,1)}, u32[]{:S(2)}) copy-start(bf16[1,96,8192]{2,1,0:T(8,128)(2,1)} %param.5) | copy-start | bytes 4718596
  7.5 15.2 %copy-start.1 = (s32[192,2]{0,1:T(2,128)S(1)}, s32[192,2]{0,1:T(2,128)}, u32[]{:S(2)}) copy-start(s32[192,2]{0,1:T(2,128)} %param.6) | copy-start | bytes 4612
  7.5 377.7 %all-to-all-start = ((bf16[64,12,8192]{2,1,0:T(8,128)(2,1)}), bf16[64,12,8192]{2,1,0:T(8,128)(2,1)}, u32[]{:S(2)}, u32[]{:S(2)}) async-start(bf16[64,12,8192]{2,1,0:T(8,128)(2,1)} %stack.3), calls=%async_computation | async-start | bytes 33554432 | tf_op jit(solution)/shard_map/all_to_all | solution.py:24
  402.0 16.7 %copy-start.2 = (f32[192,2]{0,1:T(2,128)S(1)}, f32[192,2]{0,1:T(2,128)}, u32[]{:S(2)}) copy-start(f32[192,2]{0,1:T(2,128)} %param.7) | copy-start | bytes 4612
  411.5 17.7 %all-to-all-start.1 = ((bf16[8,96,96]{1,2,0:T(8,128)(2,1)}), bf16[8,96,96]{1,2,0:T(8,128)(2,1)S(1)}, u32[]{:S(2)}, u32[]{:S(2)}) async-start(bf16[8,96,96]{1,2,0:T(8,128)(2,1)} %copy.24), calls=%async_computation.1 | async-start | bytes 393216 | tf_op jit(solution)/shard_map/all_to_all | solution.py:30
  433.4 129.8 %all-to-all-start.2 = ((bf16[8,96,96]{2,1,0:T(8,128)(2,1)}), bf16[8,96,96]{2,1,0:T(8,128)(2,1)S(1)}, u32[]{:S(2)}, u32[]{:S(2)}) async-start(bf16[8,96,96]{2,1,0:T(8,128)(2,1)} %bitcast.7), calls=%async_computation.2 | async-start | bytes 393216 | tf_op jit(solution)/shard_map/all_to_all | solution.py:43
